TPU v7x, 256 devices: a whole 4x4x8 slice. The times are simulated.
256 devices in a mesh: rows: 128 (over z, y, x), cols: 2 (over core).
Axes of the slice: x: 4, y: 4, z: 8, core: 2. Of those that a mesh axis runs over, the one named last changes fastest.
Arguments:
- design: float32 [131072, 512], P('rows', 'cols'), may hold values from -24 to 24
- signs: int32 [131072], P('rows'), may hold values from -1 to 1, as said below
- kept: int32 [8192], replicated, may hold values from 0 to 131071, as said below
Outputs:
- sketch: float32 [8192, 512], P('rows', 'cols')
- factor: float32 [512, 512], P(None, 'cols')
Inputs may be any that keep to these rules, and one draw needn't show every extreme that they name: `signs`: each entry is +1 or -1. `kept`: distinct and increasing.
All inputs are finite; a program needn't handle non-finite values.
Results may differ from a plain program's by a relative error of at most 0.0003.
Values sent between devices are 32-bit elements; how exact they have to be, the bound alone decides.
No kernel may reach another device: no remote copies, remote signals or barrier semaphores. Data moves between devices by JAX's collectives and lax.ppermute only.
A program may use at most 64 MiB of HBM per device.

v0:
```python
import math
import jax
import jax.numpy as jnp
from jax import lax
from jax.sharding import Mesh
from jax.sharding import PartitionSpec as P

ROWS = ("rows_0", "rows_1", "rows_2")


def sum_by_axis(so_far, axes):
    for axis in axes:
        so_far = lax.psum_scatter(so_far, axis, scatter_dimension=0, tiled=True)
    return so_far


def laid_out(parts, dim):
    dims = list(parts.shape[1:])
    dims[dim] *= parts.shape[0]
    return jnp.moveaxis(parts, 0, dim).reshape(dims)


def copy_for_each(shard, axis):
    length = lax.axis_size(axis)
    return lax.all_to_all(
        jnp.broadcast_to(shard[None], (length, *shard.shape)), axis, 0, 0, tiled=True
    )


def gathered_copies(shard, axis, dim):
    return laid_out(copy_for_each(shard, axis), dim)


def hadamard(order):
    matrix = jnp.ones((1, 1), jnp.float32)
    base = jnp.array([[1.0, 1.0], [1.0, -1.0]], jnp.float32)
    while matrix.shape[0] < order:
        matrix = jnp.kron(matrix, base)
    return matrix


def bit_parity(value):
    folded = value
    for amount in (16, 8, 4, 2, 1):
        folded = jnp.bitwise_xor(folded, jnp.right_shift(folded, amount))
    return jnp.bitwise_and(folded, 1)


def local_transform(flipped):
    length, width = flipped.shape
    outer = length // 128
    inner_table = hadamard(128)
    outer_table = hadamard(outer)
    blocks = flipped.reshape(outer, 128, width)
    mixed = jnp.einsum("pb,abc->apc", inner_table, blocks, precision=lax.Precision.HIGHEST)
    mixed = jnp.einsum("qa,apc->qpc", outer_table, mixed, precision=lax.Precision.HIGHEST)
    return mixed.reshape(length, width)


def signed_rows(transformed, kept_part, device_row, total_rows):
    length = transformed.shape[0]
    kept_blocks = kept_part // length
    offsets = kept_part - kept_blocks * length
    parity = bit_parity(jnp.bitwise_and(kept_blocks, device_row))
    factor = (1.0 - 2.0 * parity.astype(jnp.float32)) / math.sqrt(total_rows)
    return jnp.take(transformed, offsets, axis=0) * factor[:, None]


def body(design, signs, kept):
    flipped = design * signs.astype(jnp.float32)[:, None]
    transformed = local_transform(flipped)
    device_row = lax.axis_index(ROWS)
    groups = lax.axis_size(ROWS)
    length = transformed.shape[0]
    widths = transformed.shape[1]
    total_rows = length * groups
    sketch = sum_by_axis(signed_rows(transformed, kept, device_row, total_rows), ROWS)
    column = lax.axis_index("cols")
    whole = gathered_copies(sketch, "cols", 1)
    kept_total = kept.shape[0]
    partial_gram = jnp.dot(
        whole.T, whole, precision=lax.Precision.HIGHEST, preferred_element_type=jnp.float32
    )
    gram = lax.psum(partial_gram, ROWS) / kept_total
    factor = jnp.linalg.cholesky(gram).T
    return (sketch, lax.dynamic_slice_in_dim(factor, column * widths, widths, 1))


def solution(mesh):
    torus = Mesh(
        mesh.devices.reshape(8, 4, 4, mesh.shape["cols"]), ("rows_0", "rows_1", "rows_2", "cols")
    )
    return jax.shard_map(
        body,
        mesh=torus,
        in_specs=(P(ROWS, "cols"), P(ROWS), P()),
        out_specs=(P(ROWS, "cols"), P(None, "cols")),
        check_vma=False,
    )
```

profile of v0, /device:TPU:2, one launch (start us, length us, event | category | flops | bytes accessed | tf_op | source)
XLA Modules:
  0.0 540.0 jit_solution(2784497924892284188)
XLA Ops:
  7.2 0.0 copy-start
  7.2 0.0 reduce-scatter.4.cloned.1.call-start
  7.2 0.8 broadcast_multiply_fusion.7
  8.1 0.1 mul.255
  8.2 0.8 broadcast_multiply_fusion.6
  8.9 0.1 reshape.196
  9.0 0.1 mul.259
  9.1 0.8 broadcast_clamp_fusion
  9.9 0.8 compare_and_fusion
  10.7 0.7 convert_element_type.6
  11.4 0.8 broadcast_multiply_fusion.5
  12.1 0.1 mul.273
  12.2 0.8 broadcast_multiply_fusion.4
  13.0 0.1 mul.277
  13.1 0.9 broadcast_multiply_fusion.2
  14.0 0.6 mul.281
  14.7 3.0 broadcast_multiply_fusion
  17.7 4.0 reshape.195
  21.7 0.0 copy-done
  21.7 0.2 broadcast_multiply_fusion.3
  21.9 1.8 convolution_bitcast_fusion
  23.7 0.5 copy.15
  24.2 1.0 fusion.21
  25.2 0.3 copy.16
  25.5 0.0 copy-done.1
  25.5 0.1 fusion.19
  25.6 31.4 %gather_fusion = f32[8192,256]{1,0:T(8,128)} fusion(f32[1024,256]{1,0:T(8,128)S(1)} %bitcast.45, s32[8192]{0:T(1024)S(1)} %broadcast_clamp_fusion), kind=kCustom, calls=%fused_computation | custom fusion | bytes 16809984 | tf_op jit(solution)/shard_map/jit(_take)/gather | solution.py:66
  57.0 9.9 %select_multiply_fusion = f32[8192,256]{1,0:T(8,128)} fusion(f32[8192,256]{1,0:T(8,128)} %gather_fusion, f32[8192]{0:T(1024)S(1)} %fusion.19, pred[8192]{0:T(1024)(128)(4,1)S(1)} %compare_and_fusion), kind=kLoop, calls=%fused_computation.1 | loop fusion | flops 4194304 | bytes 16818176 | tf_op jit(solution)/shard_map/mul | solution.py:66
  66.9 0.0 reduce-scatter.4.cloned.1.call-update
  66.9 0.0 reduce-scatter.6.cloned.1.call-start
  66.9 97.9 %reduce-scatter.4.cloned.1.call-done = f32[1024,256]{1,0:T(8,128)} async-done(((f32[8192,256]{1,0:T(8,128)}), f32[1024,256]{1,0:T(8,128)}) %reduce-scatter.4.cloned.1.call-update) | async-done | bytes 1048592 | tf_op jit(solution)/shard_map/reduce_scatter | solution.py:13
  164.9 0.0 reduce-scatter.6.cloned.1.call-update
  164.9 0.0 reduce-scatter.8.cloned.1.call-start
  165.0 27.3 %reduce-scatter.6.cloned.1.call-done = f32[256,256]{1,0:T(8,128)} async-done(((f32[1024,256]{1,0:T(8,128)}), f32[256,256]{1,0:T(8,128)}) %reduce-scatter.6.cloned.1.call-update) | async-done | bytes 262160 | tf_op jit(solution)/shard_map/reduce_scatter | solution.py:13
  192.2 0.0 reduce-scatter.8.cloned.1.call-update
  192.3 0.0 all-reduce.3.cloned.1.call-start
  192.3 24.3 %reduce-scatter.8.cloned.1.call-done = f32[64,256]{1,0:T(8,128)} async-done(((f32[256,256]{1,0:T(8,128)}), f32[64,256]{1,0:T(8,128)}) %reduce-scatter.8.cloned.1.call-update) | async-done | bytes 65552 | tf_op jit(solution)/shard_map/reduce_scatter | solution.py:13
  216.6 0.8 broadcast_in_dim.59
  217.4 3.8 all_to_all.5
  221.3 2.1 fusion.22
  223.3 0.0 all-reduce.3.cloned.1.call-update
  223.4 222.7 %all-reduce.3.cloned.1.call-done = f32[512,512]{0,1:T(8,128)} async-done(((f32[512,512]{0,1:T(8,128)}), f32[512,512]{0,1:T(8,128)}) %all-reduce.3.cloned.1.call-update) | async-done | bytes 1048592 | tf_op jit(solution)/shard_map/psum | solution.py:84
  446.1 1.3 broadcast_multiply_fusion.1
  447.4 0.3 copy.19
  447.7 1.5 fusion
  449.2 11.7 %cholesky.104 = f32[128,128]{1,0:T(8,128)S(1)} custom-call(f32[128,128]{1,0:T(8,128)S(1)} %cholesky.266), custom_call_target="Cholesky" | custom-call | tf_op jit(solution)/shard_map/jit(cholesky)/cholesky | solution.py:85
  461.0 0.1 cholesky.224
  461.1 9.8 %custom-call.27 = f32[1,128,128]{1,2,0:T(8,128)S(1)} custom-call(f32[1,128,128]{2,1,0:T(8,128)S(1)} %get-tuple-element.17), custom_call_target="InvertDiagBlocksLowerTriangular" | custom-call | tf_op jit(solution)/shard_map/jit(cholesky)/cholesky | solution.py:85
  470.9 0.3 constant_dynamic-update-slice_fusion.1
  471.2 0.3 convolution_subtract_fusion
  471.6 11.7 %cholesky.217 = f32[128,128]{1,0:T(8,128)S(1)} custom-call(f32[128,128]{1,0:T(8,128)S(1)} %cholesky.270), custom_call_target="Cholesky" | custom-call | tf_op jit(solution)/shard_map/jit(cholesky)/cholesky | solution.py:85
  483.3 9.9 %custom-call.28 = f32[1,128,128]{1,2,0:T(8,128)S(1)} custom-call(f32[1,128,128]{2,1,0:T(8,128)S(1)} %get-tuple-element.14), custom_call_target="InvertDiagBlocksLowerTriangular" | custom-call | tf_op jit(solution)/shard_map/jit(cholesky)/cholesky | solution.py:85
  493.3 0.3 convolution_dynamic-update-slice_fusion
  493.6 0.4 convolution_subtract_fusion.1
  494.0 11.7 %cholesky.238 = f32[128,128]{1,0:T(8,128)S(1)} custom-call(f32[128,128]{1,0:T(8,128)S(1)} %cholesky.275), custom_call_target="Cholesky" | custom-call | tf_op jit(solution)/shard_map/jit(cholesky)/cholesky | solution.py:85
  505.7 9.8 %custom-call.29 = f32[1,128,128]{1,2,0:T(8,128)S(1)} custom-call(f32[1,128,128]{2,1,0:T(8,128)S(1)} %get-tuple-element.11), custom_call_target="InvertDiagBlocksLowerTriangular" | custom-call | tf_op jit(solution)/shard_map/jit(cholesky)/cholesky | solution.py:85
  515.5 0.2 convolution_dynamic-update-slice_fusion.1
  515.7 0.4 convolution_subtract_fusion.2
  516.1 11.7 %cholesky.255 = f32[128,128]{1,0:T(8,128)S(1)} custom-call(f32[128,128]{1,0:T(8,128)S(1)} %convolution_subtract_fusion.2), custom_call_target="Cholesky" | custom-call | tf_op jit(solution)/shard_map/jit(cholesky)/cholesky | solution.py:85
  527.9 0.7 compare_reduce_fusion.1
  528.6 0.6 compare_reduce_fusion
  529.2 0.7 compare_reduce_fusion.2
  532.4 0.1 fusion.2
  532.5 1.0 copy.20
  (9 shorter events, 0.2 us)
Async XLA Ops:
  7.2 14.5 %copy-start = (f32[1024,256]{1,0:T(8,128)S(1)}, f32[1024,256]{1,0:T(8,128)}, u32[]{:S(2)}) copy-start(f32[1024,256]{1,0:T(8,128)} %param.5) | copy-start | bytes 3145732
  7.2 157.7 %reduce-scatter.4.cloned.1.call-start = ((), (), s32[]{:S(2)}) async-start(), calls=%async_computation.4 | async-start | bytes 9437184 | tf_op jit(solution)/shard_map/reduce_scatter | solution.py:13
  17.7 7.9 %copy-start.1 = (s32[8192]{0:T(1024)S(1)}, s32[8192]{0:T(1024)}, u32[]{:S(2)}) copy-start(s32[8192]{0:T(1024)} %param.7) | copy-start | bytes 98308
  66.9 125.3 %reduce-scatter.6.cloned.1.call-start = ((), (), s32[]{:S(2)}) async-start(), calls=%async_computation.5 | async-start | bytes 1310720 | tf_op jit(solution)/shard_map/reduce_scatter | solution.py:13
  164.9 51.7 %reduce-scatter.8.cloned.1.call-start = ((), (), s32[]{:S(2)}) async-start(), calls=%async_computation.6 | async-start | bytes 327680 | tf_op jit(solution)/shard_map/reduce_scatter | solution.py:13
  192.3 253.8 %all-reduce.3.cloned.1.call-start = ((), (), s32[]{:S(2)}) async-start(), calls=%async_computation.7 | async-start | bytes 2097152 | tf_op jit(solution)/shard_map/psum | solution.py:84
Sparse Core Ops, SparseCore 0:
  67.0 97.8 reduce-scatter.3
  167.4 24.7 reduce-scatter.5
  195.5 21.0 reduce-scatter.7
  223.5 222.5 all-reduce.2
where the time goes:
time: 541 us; the launch traced here: 540 us
  waiting for transfers between devices  372 us (69%)
  other arithmetic  101 us (19%)
  local copies, waits for them, and re-layouts  39.6 us (7%)
  between operations  16.6 us (3%)
  matrix products  6.71 us (1%)
    psum x1, waiting for transfers between devices, body(): gram = lax.psum(partial_gram, ROWS) / kept_total  223 us
    reduce_scatter x3, waiting for transfers between devices, sum_by_axis(): so_far = lax.psum_scatter(so_far, axis, scatter_dimension=0, tiled=True)  149 us
    another operation x14, other arithmetic, body(): factor = jnp.linalg.cholesky(gram).T  78.6 us
    gather x1, local copies, waits for them, and re-layouts, signed_rows(): return jnp.take(transformed, offsets, axis=0) * factor[:, None]  31.4 us
  transfers between devices with their start and end apart: 4, of which 4 were waited for; matrix products, arithmetic and copies ran while one was open for 0% of the time, Pallas kernels for 0%

commit v1 on v0

--- a/solution.py
+++ b/solution.py
@@ -81,7 +81,7 @@
     partial_gram = jnp.dot(
         whole.T, whole, precision=lax.Precision.HIGHEST, preferred_element_type=jnp.float32
     )
-    gram = lax.psum(partial_gram, ROWS) / kept_total
+    gram = lax.psum(lax.psum(partial_gram, "rows_0"), ("rows_1", "rows_2")) / kept_total
     factor = jnp.linalg.cholesky(gram).T
     return (sketch, lax.dynamic_slice_in_dim(factor, column * widths, widths, 1))
 

time: 541 us -> 494 us (0.913)
  waiting for transfers between devices: 372 us -> 325 us
    psum x1 -> x2, waiting for transfers between devices: 223 us -> 175 us  [the longest x1 98.1 us: body(): lax.psum(lax.psum(partial_gram, 'rows_0'), ('rows_1', 'rows_2'))]
  transfers between devices with their start and end apart: 4 -> 5, of which waited for: 4 -> 5; matrix products, arithmetic and copies ran while one was open for 0% -> 0% of each run, Pallas kernels for 0% -> 0%
where the time goes in v1:
time: 494 us; the launch traced here: 493 us
  waiting for transfers between devices  325 us (66%)
  other arithmetic  101 us (20%)
  local copies, waits for them, and re-layouts  39.6 us (8%)
  between operations  16.6 us (3%)
  matrix products  6.7 us (1%)
    reduce_scatter x3, waiting for transfers between devices, sum_by_axis(): so_far = lax.psum_scatter(so_far, axis, scatter_dimension=0, tiled=True)  149 us
    psum x1, waiting for transfers between devices, body(): lax.psum(lax.psum(partial_gram, 'rows_0'), ('rows_1', 'rows_2'))  98.1 us
    another operation x14, other arithmetic, body(): factor = jnp.linalg.cholesky(gram).T  78.6 us
    psum x1, waiting for transfers between devices, body(): lax.psum(partial_gram, 'rows_0')  77.4 us
    gather x1, local copies, waits for them, and re-layouts, signed_rows(): return jnp.take(transformed, offsets, axis=0) * factor[:, None]  31.4 us
    mul x1, other arithmetic, signed_rows(): return jnp.take(transformed, offsets, axis=0) * factor[:, None]  9.89 us
  transfers between devices with their start and end apart: 5, of which 5 were waited for; matrix products, arithmetic and copies ran while one was open for 0% of the time, Pallas kernels for 0%

profile of v1, /device:TPU:2, one launch (start us, length us, event | category | flops | bytes accessed | tf_op | source)
XLA Modules:
  0.0 493.1 jit_solution(16199066192971871080)
XLA Ops:
  7.2 0.0 reduce-scatter.4.cloned.1.call-start
  7.2 0.8 broadcast_multiply_fusion.7
  8.1 0.1 mul.255
  8.2 0.8 broadcast_multiply_fusion.6
  8.9 0.1 reshape.196
  9.0 0.1 mul.259
  9.1 0.8 broadcast_clamp_fusion
  9.9 0.8 compare_and_fusion
  10.7 0.7 convert_element_type.6
  11.4 0.8 broadcast_multiply_fusion.5
  12.1 0.1 mul.273
  12.2 0.8 broadcast_multiply_fusion.4
  13.0 0.1 mul.277
  13.1 0.9 broadcast_multiply_fusion.2
  14.0 0.6 mul.281
  14.7 3.0 broadcast_multiply_fusion
  17.7 4.0 reshape.195
  21.7 0.2 broadcast_multiply_fusion.3
  21.9 1.8 convolution_bitcast_fusion
  23.7 0.5 copy.15
  24.2 1.0 fusion.21
  25.2 0.3 copy.16
  25.5 0.1 fusion.19
  25.6 31.4 %gather_fusion = f32[8192,256]{1,0:T(8,128)} fusion(f32[1024,256]{1,0:T(8,128)S(1)} %bitcast.45, s32[8192]{0:T(1024)S(1)} %broadcast_clamp_fusion), kind=kCustom, calls=%fused_computation | custom fusion | bytes 16809984 | tf_op jit(solution)/shard_map/jit(_take)/gather | solution.py:66
  57.0 9.9 %select_multiply_fusion = f32[8192,256]{1,0:T(8,128)} fusion(f32[8192,256]{1,0:T(8,128)} %gather_fusion, f32[8192]{0:T(1024)S(1)} %fusion.19, pred[8192]{0:T(1024)(128)(4,1)S(1)} %compare_and_fusion), kind=kLoop, calls=%fused_computation.1 | loop fusion | flops 4194304 | bytes 16818176 | tf_op jit(solution)/shard_map/mul | solution.py:66
  66.9 0.0 reduce-scatter.4.cloned.1.call-update
  66.9 0.0 reduce-scatter.6.cloned.1.call-start
  66.9 97.9 %reduce-scatter.4.cloned.1.call-done = f32[1024,256]{1,0:T(8,128)} async-done(((f32[8192,256]{1,0:T(8,128)}), f32[1024,256]{1,0:T(8,128)}) %reduce-scatter.4.cloned.1.call-update) | async-done | bytes 1048592 | tf_op jit(solution)/shard_map/reduce_scatter | solution.py:13
  164.9 0.0 reduce-scatter.6.cloned.1.call-update
  164.9 0.0 reduce-scatter.8.cloned.1.call-start
  165.0 27.3 %reduce-scatter.6.cloned.1.call-done = f32[256,256]{1,0:T(8,128)} async-done(((f32[1024,256]{1,0:T(8,128)}), f32[256,256]{1,0:T(8,128)}) %reduce-scatter.6.cloned.1.call-update) | async-done | bytes 262160 | tf_op jit(solution)/shard_map/reduce_scatter | solution.py:13
  192.2 0.0 reduce-scatter.8.cloned.1.call-update
  192.3 0.0 all-reduce.4.cloned.1.call-start
  192.3 24.3 %reduce-scatter.8.cloned.1.call-done = f32[64,256]{1,0:T(8,128)} async-done(((f32[256,256]{1,0:T(8,128)}), f32[64,256]{1,0:T(8,128)}) %reduce-scatter.8.cloned.1.call-update) | async-done | bytes 65552 | tf_op jit(solution)/shard_map/reduce_scatter | solution.py:13
  216.6 0.8 broadcast_in_dim.59
  217.4 3.8 all_to_all.5
  221.3 2.1 fusion.22
  223.3 0.0 all-reduce.4.cloned.1.call-update
  223.4 0.2 all-reduce.6.cloned.1.call-start
  223.6 77.4 %all-reduce.4.cloned.1.call-done = f32[512,512]{0,1:T(8,128)} async-done(((f32[512,512]{0,1:T(8,128)}), f32[512,512]{0,1:T(8,128)}) %all-reduce.4.cloned.1.call-update) | async-done | bytes 1048592 | tf_op jit(solution)/shard_map/psum | solution.py:84
  301.0 0.0 all-reduce.6.cloned.1.call-update
  301.0 98.1 %all-reduce.6.cloned.1.call-done = f32[512,512]{0,1:T(8,128)} async-done(((f32[512,512]{0,1:T(8,128)}), f32[512,512]{0,1:T(8,128)}) %all-reduce.6.cloned.1.call-update) | async-done | bytes 1048592 | tf_op jit(solution)/shard_map/psum | solution.py:84
  399.1 1.3 broadcast_multiply_fusion.1
  400.4 0.3 copy.19
  400.8 1.5 fusion
  402.2 11.7 %cholesky.104 = f32[128,128]{1,0:T(8,128)S(1)} custom-call(f32[128,128]{1,0:T(8,128)S(1)} %cholesky.266), custom_call_target="Cholesky" | custom-call | tf_op jit(solution)/shard_map/jit(cholesky)/cholesky | solution.py:85
  414.0 0.1 cholesky.224
  414.1 9.8 %custom-call.27 = f32[1,128,128]{1,2,0:T(8,128)S(1)} custom-call(f32[1,128,128]{2,1,0:T(8,128)S(1)} %get-tuple-element.17), custom_call_target="InvertDiagBlocksLowerTriangular" | custom-call | tf_op jit(solution)/shard_map/jit(cholesky)/cholesky | solution.py:85
  423.9 0.3 constant_dynamic-update-slice_fusion.1
  424.3 0.3 convolution_subtract_fusion
  424.6 11.7 %cholesky.217 = f32[128,128]{1,0:T(8,128)S(1)} custom-call(f32[128,128]{1,0:T(8,128)S(1)} %cholesky.270), custom_call_target="Cholesky" | custom-call | tf_op jit(solution)/shard_map/jit(cholesky)/cholesky | solution.py:85
  436.4 10.0 %custom-call.28 = f32[1,128,128]{1,2,0:T(8,128)S(1)} custom-call(f32[1,128,128]{2,1,0:T(8,128)S(1)} %get-tuple-element.14), custom_call_target="InvertDiagBlocksLowerTriangular" | custom-call | tf_op jit(solution)/shard_map/jit(cholesky)/cholesky | solution.py:85
  446.4 0.3 convolution_dynamic-update-slice_fusion
  446.6 0.4 convolution_subtract_fusion.1
  447.0 11.7 %cholesky.238 = f32[128,128]{1,0:T(8,128)S(1)} custom-call(f32[128,128]{1,0:T(8,128)S(1)} %cholesky.275), custom_call_target="Cholesky" | custom-call | tf_op jit(solution)/shard_map/jit(cholesky)/cholesky | solution.py:85
  458.8 9.8 %custom-call.29 = f32[1,128,128]{1,2,0:T(8,128)S(1)} custom-call(f32[1,128,128]{2,1,0:T(8,128)S(1)} %get-tuple-element.11), custom_call_target="InvertDiagBlocksLowerTriangular" | custom-call | tf_op jit(solution)/shard_map/jit(cholesky)/cholesky | solution.py:85
  468.6 0.2 convolution_dynamic-update-slice_fusion.1
  468.8 0.4 convolution_subtract_fusion.2
  469.2 11.7 %cholesky.255 = f32[128,128]{1,0:T(8,128)S(1)} custom-call(f32[128,128]{1,0:T(8,128)S(1)} %convolution_subtract_fusion.2), custom_call_target="Cholesky" | custom-call | tf_op jit(solution)/shard_map/jit(cholesky)/cholesky | solution.py:85
  480.9 0.7 compare_reduce_fusion.1
  481.7 0.6 compare_reduce_fusion
  482.3 0.7 compare_reduce_fusion.2
  485.5 0.1 fusion.2
  485.6 1.0 copy.20
  (12 shorter events, 0.2 us)
Async XLA Ops:
  7.2 14.5 %copy-start = (f32[1024,256]{1,0:T(8,128)S(1)}, f32[1024,256]{1,0:T(8,128)}, u32[]{:S(2)}) copy-start(f32[1024,256]{1,0:T(8,128)} %param.5) | copy-start | bytes 3145732
  7.2 157.7 %reduce-scatter.4.cloned.1.call-start = ((), (), s32[]{:S(2)}) async-start(), calls=%async_computation.4 | async-start | bytes 9437184 | tf_op jit(solution)/shard_map/reduce_scatter | solution.py:13
  17.7 7.9 %copy-start.1 = (s32[8192]{0:T(1024)S(1)}, s32[8192]{0:T(1024)}, u32[]{:S(2)}) copy-start(s32[8192]{0:T(1024)} %param.7) | copy-start | bytes 98308
  66.9 125.3 %reduce-scatter.6.cloned.1.call-start = ((), (), s32[]{:S(2)}) async-start(), calls=%async_computation.5 | async-start | bytes 1310720 | tf_op jit(solution)/shard_map/reduce_scatter | solution.py:13
  164.9 51.7 %reduce-scatter.8.cloned.1.call-start = ((), (), s32[]{:S(2)}) async-start(), calls=%async_computation.6 | async-start | bytes 327680 | tf_op jit(solution)/shard_map/reduce_scatter | solution.py:13
  192.3 108.7 %all-reduce.4.cloned.1.call-start = ((), (), s32[]{:S(2)}) async-start(), calls=%async_computation.7 | async-start | bytes 2097152 | tf_op jit(solution)/shard_map/psum | solution.py:84
  223.4 175.7 %all-reduce.6.cloned.1.call-start = ((), (), s32[]{:S(2)}) async-start(), calls=%async_computation.8 | async-start | bytes 2097152 | tf_op jit(solution)/shard_map/psum | solution.py:84
Sparse Core Ops, SparseCore 0:
  67.0 97.8 reduce-scatter.3
  167.4 24.7 reduce-scatter.5
  195.5 21.0 reduce-scatter.7
  223.5 77.4 all-reduce.3
  304.1 94.9 all-reduce.5
